TPU v7x, 1024 devices: a whole 8x8x8 slice. The times are simulated.
1024 devices in a mesh: batch: 64 (over y, z), proto: 16 (over x, core).
Axes of the slice: x: 8, y: 8, z: 8, core: 2. Of those that a mesh axis runs over, the one named last changes fastest.
Arguments:
- features: bfloat16 [8192, 1536], P('batch'), may hold values from -20 to 20
- w_first: bfloat16 [1536, 4096], P(None, 'proto'), may hold values from -0.15625 to 0.15625
- bn_gain: float32 [4096], P('proto'), may hold values from 0.1 to 1.9
- bn_shift: float32 [4096], P('proto'), may hold values from -3 to 3
- w_second: bfloat16 [4096, 256], P('proto'), may hold values from -1 to 1
- prototypes: bfloat16 [65536, 256], P('proto'), may hold values from -6 to 6
- partner: int32 [8192], P('batch'), may hold values from 0 to 127, as said below
Outputs:
- crop_penalty: float32 [8192], P('batch')
- grad_w1: float32 [1536, 4096], P('batch', 'proto')
- grad_gain: float32 [4096], P('proto')
- grad_shift: float32 [4096], P('proto')
- grad_w2: float32 [4096, 256], P('proto', 'batch')
Inputs may be any that keep to these rules, and one draw needn't show every extreme that they name: partner_i is a crop index within crop i's group of 128 consecutive crops; the partner of partner_i is i, and partner_i is never i.
All inputs are finite; a program needn't handle non-finite values.
Results may differ from a plain program's by a relative error of at most 0.015.
Values sent between devices are 32-bit elements; how exact they have to be, the bound alone decides.
A program may use at most 32 MiB of HBM per device.

v0:
```python
import jax
import jax.numpy as jnp
from jax import lax
from jax.sharding import PartitionSpec as P

ITERS = 3


balancing_epsilon = 0.05
sharpness_divisor = 0.1
penalty_weighting = 64.0


def proto_sums(values):
    return lax.psum(values, "proto")


def batch_sums(values):
    return lax.psum(values, "batch")


def body(features, w_first, bn_gain, bn_shift, w_second, prototypes, partner):
    f32 = jnp.float32
    highest = lax.Precision.HIGHEST
    crop_rows = features.shape[0]
    crops_all = crop_rows * lax.axis_size("batch")
    pre_act = jnp.dot(features, w_first, preferred_element_type=f32)
    first_moment, second_moment = batch_sums((jnp.sum(pre_act, 0), jnp.sum(pre_act * pre_act, 0)))
    batch_mean = first_moment / crops_all
    batch_var = second_moment / crops_all - batch_mean * batch_mean
    inv_std = lax.rsqrt(batch_var + 1e-05)
    normed = (pre_act - batch_mean) * inv_std
    shifted = bn_gain * normed + bn_shift
    hidden = jnp.maximum(shifted, 0.0).astype(jnp.bfloat16)
    raw_emb = proto_sums(jnp.dot(hidden, w_second, preferred_element_type=f32))
    inv_norm = lax.rsqrt(jnp.sum(raw_emb * raw_emb, 1, keepdims=True) + 1e-06)
    embedded = raw_emb * inv_norm
    emb_low = embedded.astype(jnp.bfloat16)
    proto_float = prototypes.astype(f32)
    unit_protos = (
        proto_float * lax.rsqrt(jnp.sum(proto_float * proto_float, 1, keepdims=True) + 1e-06)
    ).astype(jnp.bfloat16)
    centroid_affinity = lax.dot_general(
        emb_low, unit_protos, (((1,), (1,)), ((), ())), preferred_element_type=f32
    )
    exponent_codes = jnp.exp(centroid_affinity / balancing_epsilon)
    raised_affinity = jnp.exp(centroid_affinity / sharpness_divisor)
    part_total = jnp.sum(raised_affinity, 1)
    scale_rows = jnp.ones((crop_rows,), f32)
    for iteration in range(ITERS):
        col_part = jnp.dot(scale_rows, exponent_codes, precision=highest)
        scale_cols = 1.0 / batch_sums(col_part)
        scale_rows = 1.0 / proto_sums(jnp.dot(exponent_codes, scale_cols, precision=highest))
    partner_codes = jnp.take(exponent_codes, partner, axis=0) * scale_cols
    cross_part = jnp.sum(partner_codes * centroid_affinity, 1)
    partition_total, mismatch_total = proto_sums((part_total, cross_part))
    companion_weighting = jnp.take(scale_rows, partner)
    crop_penalty = (
        jnp.log(partition_total) - companion_weighting * mismatch_total / sharpness_divisor
    )
    desired_assignments = partner_codes * companion_weighting[:, None]
    normalized_likelihood = raised_affinity / partition_total[:, None]
    affinity_derivative = (
        penalty_weighting * (normalized_likelihood - desired_assignments) / sharpness_divisor
    ).astype(jnp.bfloat16)
    emb_grad = proto_sums(jnp.dot(affinity_derivative, unit_protos, preferred_element_type=f32))
    inner_prod = jnp.sum(embedded * emb_grad, 1, keepdims=True)
    raw_grad = ((emb_grad - embedded * inner_prod) * inv_norm).astype(jnp.bfloat16)
    second_local = lax.dot_general(
        hidden, raw_grad, (((0,), (0,)), ((), ())), preferred_element_type=f32
    )
    hidden_grad = lax.dot_general(
        raw_grad, w_second, (((1,), (1,)), ((), ())), preferred_element_type=f32
    )
    bn_grad = jnp.where(shifted > 0, hidden_grad, 0.0)
    grad_shift, grad_gain = batch_sums((jnp.sum(bn_grad, 0), jnp.sum(bn_grad * normed, 0)))
    pre_grad = (
        bn_gain * inv_std * (bn_grad - grad_shift / crops_all - normed * grad_gain / crops_all)
    ).astype(jnp.bfloat16)
    first_local = lax.dot_general(
        features, pre_grad, (((0,), (0,)), ((), ())), preferred_element_type=f32
    )
    grad_w1, grad_w2 = (
        lax.psum_scatter(first_local, "batch", scatter_dimension=0, tiled=True),
        lax.psum_scatter(second_local, "batch", scatter_dimension=1, tiled=True),
    )
    return (crop_penalty, grad_w1, grad_gain, grad_shift, grad_w2)


def solution(mesh):
    return jax.shard_map(
        body,
        mesh=mesh,
        in_specs=(
            P("batch", None),
            P(None, "proto"),
            P("proto"),
            P("proto"),
            P("proto", None),
            P("proto", None),
            P("batch"),
        ),
        out_specs=(P("batch"), P("batch", "proto"), P("proto"), P("proto"), P("proto", "batch")),
        check_vma=False,
    )
```

profile of v0, /device:TPU:1, one launch (start us, length us, event | category | flops | bytes accessed | tf_op | source)
XLA Modules:
  0.0 1655.7 jit_solution(4681207666346424297)
XLA Ops:
  7.2 0.0 all-reduce.10.cloned.1.call-start
  7.2 1.1 copy-done
  8.3 1.3 fusion.35
  9.6 130.0 %all-reduce.3 = (f32[256]{0:T(256)S(1)}, f32[256]{0:T(256)S(1)}) all-reduce(f32[256]{0:T(256)S(1)} %get-tuple-element.25, f32[256]{0:T(256)S(1)} %get-tuple-element.24), channel_id=1, replica_groups=mesh['batch'=64,'proto'=16] {'batch'}, use_global_device_ids=true, to_apply=%region_3.0 | all-reduce | flops 512 | bytes 4096 | tf_op jit(solution)/shard_map/psum | solution.py:19
  139.6 1.3 fusion.14
  140.9 0.5 copy-done.6
  141.4 1.7 fusion.33
  143.2 0.0 all-reduce.10.cloned.1.call-update
  143.2 0.0 all-reduce.12.cloned.1.call-start
  143.2 0.7 compare_and_fusion
  143.9 0.7 compare_select_fusion
  144.6 2.2 fusion
  146.8 135.3 %all-reduce.10.cloned.1.call-done = f32[128,256]{1,0:T(8,128)} async-done(((f32[128,256]{1,0:T(8,128)}), f32[128,256]{1,0:T(8,128)}) %all-reduce.10.cloned.1.call-update) | async-done | bytes 131088 | tf_op jit(solution)/shard_map/psum | solution.py:15
  282.1 1.0 multiply_reduce_fusion.3
  283.2 2.4 multiply_exponential_fusion
  285.6 1.3 copy-done.1
  286.9 1.3 fusion.21
  288.2 226.3 %psum.102 = f32[4096]{0:T(1024)S(1)} all-reduce(f32[4096]{0:T(1024)S(1)} %bitcast.38), channel_id=1, replica_groups=mesh['batch'=64,'proto'=16] {'batch'}, use_global_device_ids=true, to_apply=%region_9.0 | all-reduce | flops 4096 | bytes 32768 | tf_op jit(solution)/shard_map/psum | solution.py:19
  514.5 3.4 convolution_bitcast_fusion.3
  517.9 78.7 %psum.103 = f32[128]{0:T(128)S(1)} all-reduce(f32[128]{0:T(128)S(1)} %convolution_bitcast_fusion.3), channel_id=1, replica_groups=mesh['batch'=64,'proto'=16] {'proto'}, use_global_device_ids=true, to_apply=%region_10.0 | all-reduce | flops 128 | bytes 1024 | tf_op jit(solution)/shard_map/psum | solution.py:15
  596.6 2.9 fusion.17
  599.5 218.9 %psum.104 = f32[4096]{0:T(1024)S(1)} all-reduce(f32[4096]{0:T(1024)S(1)} %bitcast.35), channel_id=1, replica_groups=mesh['batch'=64,'proto'=16] {'batch'}, use_global_device_ids=true, to_apply=%region_11.0 | all-reduce | flops 4096 | bytes 32768 | tf_op jit(solution)/shard_map/psum | solution.py:19
  818.5 3.4 convolution_bitcast_fusion.2
  821.9 78.6 %psum.105 = f32[128]{0:T(128)S(1)} all-reduce(f32[128]{0:T(128)S(1)} %convolution_bitcast_fusion.2), channel_id=1, replica_groups=mesh['batch'=64,'proto'=16] {'proto'}, use_global_device_ids=true, to_apply=%region_12.0 | all-reduce | flops 128 | bytes 1024 | tf_op jit(solution)/shard_map/psum | solution.py:15
  900.4 2.9 fusion.15
  903.3 219.1 %psum.106 = f32[4096]{0:T(1024)S(1)} all-reduce(f32[4096]{0:T(1024)S(1)} %bitcast.37), channel_id=1, replica_groups=mesh['batch'=64,'proto'=16] {'batch'}, use_global_device_ids=true, to_apply=%region_13.0 | all-reduce | flops 4096 | bytes 32768 | tf_op jit(solution)/shard_map/psum | solution.py:19
  1122.4 3.4 convolution_bitcast_fusion.1
  1125.8 2.6 gather_fusion.1
  1128.4 3.0 fusion.2
  1131.4 78.5 %all-reduce.5 = (f32[128]{0:T(128)S(1)}, f32[128]{0:T(128)S(1)}, f32[128]{0:T(128)S(1)}) all-reduce(f32[128]{0:T(128)S(1)} %convolution_bitcast_fusion.1, f32[128]{0:T(128)S(1)} %get-tuple-element.21, f32[128]{0:T(128)S(1)} %get-tuple-element.20), channel_id=1, replica_groups=mesh['batch'=64,'proto'=16] {'proto'}, use_global_device_ids=true, to_apply=%region_14.15 | all-reduce | flops 384 | bytes 3072 | tf_op jit(solution)/shard_map/psum | solution.py:15
  1210.0 1.2 gather_fusion
  1211.2 0.5 multiply_subtract_fusion
  1211.8 4.1 fusion.3
  1215.9 0.0 all-reduce.12.cloned.1.call-update
  1215.9 0.0 all-reduce.14.cloned.1.call-start
  1216.0 111.6 %all-reduce.12.cloned.1.call-done = f32[128,256]{1,0:T(8,128)} async-done(((f32[128,256]{1,0:T(8,128)}), f32[128,256]{1,0:T(8,128)}) %all-reduce.12.cloned.1.call-update) | async-done | bytes 131088 | tf_op jit(solution)/shard_map/psum | solution.py:15
  1327.6 1.1 multiply_reduce_fusion.2
  1328.7 1.0 multiply_convert_fusion.3
  1329.7 1.2 fusion.34
  1330.9 1.7 fusion.32
  1332.5 117.7 %all-reduce.2 = (f32[256]{0:T(256)S(1)}, f32[256]{0:T(256)S(1)}) all-reduce(f32[256]{0:T(256)S(1)} %get-tuple-element.23, f32[256]{0:T(256)S(1)} %get-tuple-element.22), channel_id=1, replica_groups=mesh['batch'=64,'proto'=16] {'batch'}, use_global_device_ids=true, to_apply=%region_22.23 | all-reduce | flops 512 | bytes 4096 | tf_op jit(solution)/shard_map/psum | solution.py:19
  1450.2 2.2 convolution_bitcast_fusion
  1452.5 0.0 all-reduce.14.cloned.1.call-update
  1452.5 1.3 dynamic-slice
  1455.1 191.0 %all-reduce.14.cloned.1.call-done = (f32[1536,256]{0,1:T(8,128)}, f32[256,256]{0,1:T(8,128)}) async-done(((f32[1536,256]{0,1:T(8,128)}, f32[256,256]{0,1:T(8,128)}), (f32[1536,256]{0,1:T(8,128)}, f32[256,256]{0,1:T(8,128)})) %all-reduce.14.cloned.1.call-update) | async-done | bytes 1835024
  1646.1 1.0 constant_dynamic-slice_fusion.1
  1647.2 0.7 copy.14
  1647.9 1.3 constant_dynamic-slice_fusion
  (33 shorter events, 0.1 us)
Async XLA Ops:
  7.2 1.1 copy-start
  7.2 274.9 %all-reduce.10.cloned.1.call-start = ((), (), s32[]{:S(2)}) async-start(), calls=%async_computation | async-start | bytes 262144 | tf_op jit(solution)/shard_map/psum | solution.py:15
  140.9 0.5 copy-start.6
  140.9 0.5 copy-start.7
  143.2 1184.4 %all-reduce.12.cloned.1.call-start = ((), (), s32[]{:S(2)}) async-start(), calls=%async_computation.1 | async-start | bytes 262144 | tf_op jit(solution)/shard_map/psum | solution.py:15
  143.9 984.5 %copy-start.11 = (pred[128]{0:T(512)(128)(4,1)}, pred[128]{0:T(512)(128)(4,1)S(1)}, u32[]{:S(2)}) copy-start(pred[128]{0:T(512)(128)(4,1)S(1)} %compare_and_fusion) | copy-start | bytes 388
  146.8 138.8 %copy-start.5 = (f32[4096]{0:T(1024)}, f32[4096]{0:T(1024)S(1)}, u32[]{:S(2)}) copy-start(f32[4096]{0:T(1024)S(1)} %add_rsqrt_fusion) | copy-start | bytes 49156
  283.1 2.5 copy-start.8
  285.6 1.3 copy-start.1
  1128.4 82.8 %copy-start.12 = (s32[128]{0:T(128)S(1)}, s32[128]{0:T(128)}, u32[]{:S(2)}) copy-start(s32[128]{0:T(128)} %param.13) | copy-start | bytes 1540
  1128.4 83.3 %copy-start.2 = (f32[128,4096]{1,0:T(8,128)S(1)}, f32[128,4096]{1,0:T(8,128)}, u32[]{:S(2)}) copy-start(f32[128,4096]{1,0:T(8,128)} %copy-done.1) | copy-start | bytes 6291460
  1210.0 1.8 copy-start.13
  1211.8 115.8 %copy-start.3 = (f32[128,256]{1,0:T(8,128)S(1)}, f32[128,256]{1,0:T(8,128)}, u32[]{:S(2)}) copy-start(f32[128,256]{1,0:T(8,128)} %all-reduce.10.cloned.1.call-done) | copy-start | bytes 393220
  1211.8 238.5 %copy-start.4 = (bf16[128,1536]{1,0:T(8,128)(2,1)S(1)}, bf16[128,1536]{1,0:T(8,128)(2,1)}, u32[]{:S(2)}) copy-start(bf16[128,1536]{1,0:T(8,128)(2,1)} %param.7) | copy-start | bytes 1179652
  1215.9 430.2 %all-reduce.14.cloned.1.call-start = ((), (), s32[]{:S(2)}) async-start(), calls=%async_computation.2 | async-start | bytes 3670016
  1450.2 196.9 %copy-start.9 = (f32[256]{0:T(256)}, f32[256]{0:T(256)S(1)}, u32[]{:S(2)}) copy-start(f32[256]{0:T(256)S(1)} %get-tuple-element.26) | copy-start | bytes 3076
  1450.2 197.0 %copy-start.10 = (f32[256]{0:T(256)}, f32[256]{0:T(256)S(1)}, u32[]{:S(2)}) copy-start(f32[256]{0:T(256)S(1)} %get-tuple-element.27) | copy-start | bytes 3076
Sparse Core Ops, SparseCore 0:
  143.3 138.7 all-reduce.9
  1216.0 111.4 all-reduce.11
  1452.6 193.4 all-reduce.13
where the time goes:
time: 1660 us
  blocking collectives  1150 us (69%)
  waiting for transfers between devices  438 us (26%)
  matrix products  31.9 us (2%)
    psum x5, blocking collectives, batch_sums(): return lax.psum(values, 'batch')  912 us
    psum x2, waiting for transfers between devices, proto_sums(): return lax.psum(values, 'proto')  247 us
    psum x3, blocking collectives, proto_sums(): return lax.psum(values, 'proto')  236 us
    unnamed x4, waiting for transfers between devices  191 us
  transfers between devices with their start and end apart: 3, of which 3 were waited for; matrix products, arithmetic and copies ran while one was open for 0% of the time, Pallas kernels for 0%

commit v1 on v0

v1 whole, which is shorter than its diff:
```python
from types import SimpleNamespace

import jax
import jax.numpy as jnp
from jax import lax
from jax.experimental import pallas as pl
from jax.experimental.pallas import tpu as pltpu
from jax.sharding import PartitionSpec as P

ITERS = 3
MESH = pl.DeviceIdType.MESH
f32, bf16 = jnp.float32, jnp.bfloat16
CONTRACT_LAST = (((1,), (1,)), ((), ()))
CONTRACT_FIRST = (((0,), (0,)), ((), ()))

penalty_weighting = 64.0


def total(ref):
    count = ref.shape[0]
    chains = 4 if count >= 16 else 1
    sums = [ref[chain] for chain in range(chains)]
    for slot in range(chains, count):
        sums[slot % chains] = sums[slot % chains] + ref[slot]
    while len(sums) > 1:
        sums = [sums[i] + sums[i + 1] for i in range(0, len(sums), 2)]
    return sums[0]


def split(value):
    high = value.astype(bf16)
    low = (value - high.astype(f32)).astype(bf16)
    return jnp.concatenate([high, low], 0)


def make_kernel(ny, nz, npr, names, crops_all):
    def kernel(*refs):
        r = SimpleNamespace(**dict(zip(names, refs)))
        batch, proto = lax.axis_index("batch"), lax.axis_index("proto")
        y, z = batch // nz, batch % nz
        rings = {
            "y": (ny, y, lambda q: (q * nz + z, proto)),
            "z": (nz, z, lambda q: (y * nz + q, proto)),
            "p": (npr, proto, lambda q: (batch, q)),
        }
        send_sem, recv_sem, in_sem = r.send_sem, r.recv_sem, r.in_sem
        stages = []

        def send(source, target, stage, device):
            pltpu.make_async_remote_copy(
                src_ref=source,
                dst_ref=target,
                send_sem=send_sem.at[stage],
                recv_sem=recv_sem.at[stage],
                device_id=device,
                device_id_type=MESH,
            ).start()

        def new_stage(part):
            stages.append(part)
            return len(stages) - 1

        def exchange(axis, source_of, landing):
            count, me, device = rings[axis]
            stage = new_stage(landing.at[pl.ds(0, count - 1)])

            def step(offset, carry):
                peer = (me + offset) % count
                send(source_of(peer), landing.at[me], stage, device(peer))
                return carry

            lax.fori_loop(1, count, step, 0)
            landing[me] = source_of(me)[...]
            return stage

        def arrived(stage):
            pltpu.make_async_copy(stages[stage], stages[stage], recv_sem.at[stage]).wait()

        def sent(stage):
            pltpu.make_async_copy(stages[stage], stages[stage], send_sem.at[stage]).wait()

        def scatter(axis, source, landing, relay):
            count, me, device = rings[axis]
            far = count // 2
            stage_r, stage = new_stage(relay), new_stage(landing)
            back = (me + count - 1) % count
            send(source.at[(me + far) % count], relay, stage_r, device(back))
            near = [o for d in range(far - 1, 0, -1) for o in (d, count - d) if o != far + 1]
            for slot, offset in enumerate(near):
                peer = (me + offset) % count
                send(source.at[peer], landing.at[slot], stage, device(peer))

            def pass_on():
                arrived(stage_r)
                peer = (me + far + 1) % count
                source[peer] = source[peer] + relay[...]
                send(source.at[peer], landing.at[len(near)], stage, device(peer))

            def result():
                arrived(stage)
                return total(landing) + source[me]

            return pass_on, result

        loads = [
            pltpu.make_async_copy(src, dst, in_sem.at[i])
            for i, (src, dst) in enumerate(
                (
                    (r.f_in, r.f),
                    (r.w1_in, r.w1),
                    (r.w2_in, r.w2),
                    (r.pr_in, r.pr),
                    (r.gain_in, r.gain),
                    (r.shift_in, r.shift),
                    (r.partner_in, r.partner),
                )
            )
        ]
        for load in loads:
            load.start()

        barrier = pltpu.get_barrier_semaphore()
        peers = 0
        for axis in ("y", "z", "p"):
            count, me, device = rings[axis]
            peers += count - 1

            def greet(offset, carry, count=count, me=me, device=device):
                pl.semaphore_signal(
                    barrier, inc=1, device_id=device((me + offset) % count), device_id_type=MESH
                )
                return carry

            lax.fori_loop(1, count, greet, 0)

        loads[0].wait()
        loads[1].wait()
        pre_act = jnp.dot(r.f[...], r.w1[...], preferred_element_type=f32)
        r.pre[...] = pre_act
        r.mom[0:1, :] = jnp.sum(pre_act, 0, keepdims=True)
        r.mom[1:2, :] = jnp.sum(pre_act * pre_act, 0, keepdims=True)
        pl.semaphore_wait(barrier, peers)
        stage = exchange("y", lambda q: r.mom, r.mom_y)
        r.fsum[...] = jnp.sum(r.f[...].astype(f32), 0, keepdims=True)
        stage_f = exchange("y", lambda q: r.fsum, r.fsum_y)
        rows, emb = r.f.shape[0], r.w2.shape[1]
        lanes = 128
        slab, piece = r.ft.shape[1], r.grad_w1.shape[0]
        features_t = r.f[...].astype(f32).T.astype(bf16).reshape(ny, slab, rows)
        r.ft[:, :, :rows] = features_t
        r.ft[:, :, rows:] = features_t
        arrived(stage)
        r.mom2[...] = total(r.mom_y)
        stage = exchange("z", lambda q: r.mom2, r.mom_z)

        def by_features(right, left_out, right_out):
            def step(i, carry):
                grad = jnp.dot(r.ft[i], right[...], preferred_element_type=f32)
                left_out[i] = grad[:, :lanes].reshape(nz, piece, lanes)
                for q in range(nz):
                    right_out[q, i] = grad[q * piece : (q + 1) * piece, lanes:]
                return carry

            lax.fori_loop(0, ny, step, 0)

        r.pair[0] = split(r.pre[...])
        by_features(r.pair.at[0], r.fna, r.fnb)
        pass_a, early_a = scatter("y", r.fna, r.fna_y, r.fna_r)
        pass_b, early_b = scatter("z", r.fnb, r.fnb_z, r.fnb_r)
        for load in loads[2:]:
            load.wait()
        arrived(stage)
        moments = total(r.mom_z)
        batch_mean = moments[0:1, :] / crops_all
        batch_var = moments[1:2, :] / crops_all - batch_mean * batch_mean
        inv_std = lax.rsqrt(batch_var + 1e-05)
        gain, shift = r.gain[...], r.shift[...]
        normed = (r.pre[...] - batch_mean) * inv_std
        shifted = gain * normed + shift
        hidden = jnp.maximum(shifted, 0.0).astype(bf16)
        r.normed[...] = normed
        r.shifted[...] = shifted
        r.hidden[...] = hidden

        part = jnp.dot(hidden, r.w2[...], preferred_element_type=f32)
        r.emb_part[...] = part.reshape(r.emb_part.shape)
        stage = exchange("p", lambda q: r.emb_part.at[q], r.emb_rs)

        chunks, width = r.u.shape[0], r.u.shape[1]

        def unit(j, carry):
            proto_float = r.pr[j].astype(f32)
            inv = lax.rsqrt(jnp.sum(proto_float * proto_float, 1, keepdims=True) + 1e-06)
            r.u[j] = (proto_float * inv).astype(bf16)
            return carry

        lax.fori_loop(0, chunks // 2, unit, 0)
        pass_a()
        pass_b()
        arrived(stage)
        r.emb_own[...] = total(r.emb_rs)
        stage = exchange("p", lambda q: r.emb_own, r.emb_ag)
        lax.fori_loop(chunks // 2, chunks, unit, 0)
        arrived(stage_f)
        r.fsum2[...] = total(r.fsum_y)
        stage_f = exchange("z", lambda q: r.fsum2, r.fsum_z)
        arrived(stage)
        raw_emb = r.emb_ag[...].reshape(rows, emb)
        inv_norm = lax.rsqrt(jnp.sum(raw_emb * raw_emb, 1, keepdims=True) + 1e-06)
        embedded = raw_emb * inv_norm
        emb_low = embedded.astype(bf16)
        r.embedded[...] = embedded
        r.emb_low[...] = emb_low
        r.inv_norm[...] = jnp.broadcast_to(inv_norm, r.inv_norm.shape)

        half = width // 2
        groups = width // lanes

        def columns(j, codes):
            mass = jnp.sum(codes, 0, keepdims=True)
            r.col_a[0, pl.ds(j, 1), :] = mass[:, :half]
            r.col_b[0, pl.ds(j, 1), :] = mass[:, half:]

        def score(j, acc):
            affinity = lax.dot_general(
                r.emb_low[...], r.u[j], CONTRACT_LAST, preferred_element_type=f32
            )
            raised = jnp.exp(affinity * 10.0)
            codes = raised * raised
            r.codes[j] = codes
            r.raised[j] = raised.astype(bf16)
            columns(j, codes)
            for g in range(groups):
                acc = acc + raised[:, g * lanes : (g + 1) * lanes]
            return acc

        denom_part = lax.fori_loop(0, chunks, score, jnp.zeros((rows, lanes), f32))

        def to_row(square):
            return jnp.sum(square.T, 0, keepdims=True)

        def to_columns(row):
            return jnp.broadcast_to(row, (rows, lanes)).T

        def row_sums(scale):
            def step(j, acc):
                codes = r.codes[j]
                weight_a = codes[:, :half] * r.scale_a[pl.ds(j, 1), :]
                weight_b = codes[:, half:] * r.scale_b[pl.ds(j, 1), :]
                for g in range(half // lanes):
                    acc = acc + weight_a[:, g * lanes : (g + 1) * lanes]
                    acc = acc + weight_b[:, g * lanes : (g + 1) * lanes]
                return acc

            return to_row(lax.fori_loop(0, chunks, step, jnp.zeros((rows, lanes), f32)))

        for it in range(ITERS):
            stage_a = exchange("y", lambda q: r.col_a.at[it], r.col_a1.at[it])
            stage_b = exchange("z", lambda q: r.col_b.at[it], r.col_b1.at[it])
            if it == 0:
                def soft(j, acc):
                    return acc + jnp.dot(r.raised[j], r.u[j], preferred_element_type=f32)

                soft_part = lax.fori_loop(0, chunks, soft, jnp.zeros((rows, emb), f32))
                r.soft_part[...] = soft_part.reshape(r.soft_part.shape)
                soft_rs = exchange("p", lambda q: r.soft_part.at[q], r.soft_rs)
                r.row_src[0, 1:2, :] = to_row(denom_part)
            if it == 1:
                arrived(soft_rs)
                r.soft_own[...] = total(r.soft_rs)
                soft_ag = exchange("p", lambda q: r.soft_own, r.soft_ag)
                r.row_src[1, 1:2, :] = jnp.zeros((1, lanes), f32)
                arrived(stage_f)
                wanted = batch * piece + lax.broadcasted_iota(jnp.int32, (piece, ny * slab), 0)
                here = lax.broadcasted_iota(jnp.int32, (piece, ny * slab), 1) == wanted
                r.fsum_own[...] = jnp.broadcast_to(
                    jnp.sum(jnp.where(here, total(r.fsum_z), 0.0), 1, keepdims=True), (piece, lanes)
                )
                r.fnas[...] = early_a()
                stage_na = exchange("z", lambda q: r.fnas.at[q], r.fna_z)
                r.fnbs[...] = early_b()
                stage_nb = exchange("y", lambda q: r.fnbs.at[q], r.fnb_y)
            if it == 2:
                arrived(stage_na)
                r.fn_own[:, :lanes] = total(r.fna_z)
                arrived(stage_nb)
                r.fn_own[:, lanes:] = total(r.fnb_y)
            arrived(stage_a)
            r.col_as[it] = total(r.col_a1.at[it])
            stage_a = exchange("z", lambda q: r.col_as.at[it], r.col_a2.at[it])
            arrived(stage_b)
            r.col_bs[it] = total(r.col_b1.at[it])
            stage_b = exchange("y", lambda q: r.col_bs.at[it], r.col_b2.at[it])
            arrived(stage_a)
            r.scale_a[...] = 1.0 / total(r.col_a2.at[it])
            arrived(stage_b)
            r.scale_b[...] = 1.0 / total(r.col_b2.at[it])
            if it == ITERS - 1:
                break
            r.row_src[it, 0:1, :] = row_sums(None)
            stage = exchange("p", lambda q: r.row_src.at[it], r.row_ag.at[it])
            arrived(stage)
            masses = total(r.row_ag.at[it])
            if it == 0:
                r.denom[...] = masses[1:2, :]
            r.scale_rows[...] = to_columns(1.0 / masses[0:1, :])

            def column_sums(j, carry):
                scale = r.scale_rows[...]
                masses = [
                    jnp.sum(r.codes[j, :, g * lanes : (g + 1) * lanes] * scale, 0, keepdims=True)
                    for g in range(groups)
                ]
                r.col_a[it + 1, pl.ds(j, 1), :] = jnp.concatenate(masses[: groups // 2], 1)
                r.col_b[it + 1, pl.ds(j, 1), :] = jnp.concatenate(masses[groups // 2 :], 1)
                return carry

            lax.fori_loop(0, chunks, column_sums, 0)

        def target(j, carry):
            acc, grad = carry
            codes = r.codes[j]
            weight_a = codes[:, :half] * r.scale_a[pl.ds(j, 1), :]
            weight_b = codes[:, half:] * r.scale_b[pl.ds(j, 1), :]
            for g in range(half // lanes):
                acc = acc + weight_a[:, g * lanes : (g + 1) * lanes]
                acc = acc + weight_b[:, g * lanes : (g + 1) * lanes]
            grad = grad + jnp.dot(
                weight_a.astype(bf16), r.u[j, :half], preferred_element_type=f32
            )
            grad = grad + jnp.dot(
                weight_b.astype(bf16), r.u[j, half:], preferred_element_type=f32
            )
            return acc, grad

        row_part, target_part = lax.fori_loop(
            0, chunks, target, (jnp.zeros((rows, lanes), f32), jnp.zeros((rows, emb), f32))
        )
        r.tgt_part[...] = target_part.reshape(r.tgt_part.shape)
        stage = exchange("p", lambda q: r.tgt_part.at[q], r.tgt_rs)
        r.row_last[...] = to_row(row_part)
        stage_r = exchange("p", lambda q: r.row_last, r.row_last_ag)
        arrived(stage)
        r.tgt_own[...] = total(r.tgt_rs)
        stage = exchange("p", lambda q: r.tgt_own, r.tgt_ag)
        arrived(soft_ag)
        arrived(stage_r)
        scale_last = to_columns(1.0 / total(r.row_last_ag))
        denom = r.denom[...]
        denom_columns = to_columns(1.0 / denom)
        rows_iota = lax.broadcasted_iota(jnp.int32, (rows, rows), 0)
        swap = jnp.where(r.partner[...] == rows_iota, 1.0, 0.0).astype(f32)
        wide = lambda x: jnp.concatenate([x, x], 1)
        soft_grad = r.soft_ag[...].reshape(rows, emb) * wide(denom_columns)
        arrived(stage)
        own_target = r.tgt_ag[...].reshape(rows, emb) * wide(scale_last)
        partner_target = jnp.dot(
            swap, own_target, precision=lax.Precision.HIGHEST, preferred_element_type=f32
        )
        emb_grad = (soft_grad - partner_target) * (penalty_weighting * 10.0)
        embedded = r.embedded[...]
        inner = jnp.sum(embedded * emb_grad, 1, keepdims=True)
        raw_grad = ((emb_grad - embedded * inner) * r.inv_norm[:, 0:1]).astype(bf16)

        hidden_grad = lax.dot_general(
            raw_grad, r.w2[...], CONTRACT_LAST, preferred_element_type=f32
        )
        bn_grad = jnp.where(r.shifted[...] > 0, hidden_grad, 0.0)
        r.gsum[0:1, :] = jnp.sum(bn_grad, 0, keepdims=True)
        r.gsum[1:2, :] = jnp.sum(bn_grad * r.normed[...], 0, keepdims=True)
        stage = exchange("y", lambda q: r.gsum, r.gsum_y)
        r.pair[1] = split(bn_grad)
        by_features(r.pair.at[1], r.g1a, r.g1b)
        pass_a, late_a = scatter("y", r.g1a, r.g1a_y, r.g1a_r)
        pass_b, late_b = scatter("z", r.g1b, r.g1b_z, r.g1b_r)
        w2_grad = lax.dot_general(
            raw_grad, r.hidden[...], CONTRACT_FIRST, preferred_element_type=f32
        )
        r.g2a[...] = w2_grad[:, :lanes].reshape(ny, nz // 2, 8, lanes)
        right = w2_grad[:, lanes:].reshape(ny // 2, 2, nz // 2, 8, lanes)
        upper = lax.broadcasted_iota(jnp.int32, (nz // 2, 8, lanes), 1) < 4
        for i in range(ny // 2):
            one, two = right[i, 0], right[i, 1]
            r.g2b[:, 0, i] = jnp.where(upper, one, pltpu.roll(two, 4, 1))
            r.g2b[:, 1, i] = jnp.where(upper, pltpu.roll(one, 4, 1), two)
        stage_2a = exchange("y", lambda q: r.g2a.at[q], r.g2a_y)
        stage_2b = exchange("z", lambda q: r.g2b.at[q // 2, q % 2], r.g2b_z)
        score_dot = r.emb_low[...].astype(f32) * partner_target
        mismatch = to_row(score_dot[:, :lanes] + score_dot[:, lanes:])
        r.penalty[...] = jnp.log(denom) - mismatch * 10.0
        arrived(stage)
        r.gsum2[...] = total(r.gsum_y)
        stage = exchange("z", lambda q: r.gsum2, r.gsum_z)
        pass_a()
        pass_b()
        arrived(stage)
        sums = total(r.gsum_z)
        grad_shift, grad_gain = sums[0:1, :], sums[1:2, :]
        r.grad_shift[...] = grad_shift
        r.grad_gain[...] = grad_gain
        scale = gain * inv_std
        fsum = jnp.concatenate([r.fsum_own[...], r.fsum_own[...]], 1)
        by_normed = (r.fn_own[...] - fsum * batch_mean) * inv_std
        known = fsum * (grad_shift / crops_all) + by_normed * (grad_gain / crops_all)
        arrived(stage_2a)
        r.g2as[...] = total(r.g2a_y)
        stage_2a = exchange("z", lambda q: r.g2as.at[q // 2], r.g2a_z)
        arrived(stage_2b)
        r.g2bs[...] = total(r.g2b_z)
        stage_2b = exchange("y", lambda q: r.g2bs.at[q // 2], r.g2b_y)
        r.g1as[...] = late_a()
        stage_a = exchange("z", lambda q: r.g1as.at[q], r.g1a_z)
        r.g1bs[...] = late_b()
        stage_b = exchange("y", lambda q: r.g1bs.at[q], r.g1b_y)

        def own_half(tile, place):
            return jnp.where(place % 2 == 1, pltpu.roll(tile, 4, 0), tile)[0:4]

        arrived(stage_2a)
        r.grad_w2[:, :lanes] = own_half(total(r.g2a_z), z)
        arrived(stage_2b)
        r.grad_w2[:, lanes:] = own_half(total(r.g2b_y), y)
        arrived(stage_a)
        r.grad_w1[:, :lanes] = scale[:, :lanes] * (total(r.g1a_z) - known[:, :lanes])
        arrived(stage_b)
        r.grad_w1[:, lanes:] = scale[:, lanes:] * (total(r.g1b_y) - known[:, lanes:])
        for stage in range(len(stages)):
            sent(stage)

    return kernel


def hand_over(*refs):
    count = len(refs) // 2
    copies = [pltpu.make_async_copy(refs[i], refs[count + i], refs[-1].at[i]) for i in range(count)]
    for copy in copies:
        copy.start()
    for copy in copies:
        copy.wait()


def solution(mesh):
    nb, npr = mesh.shape["batch"], mesh.shape["proto"]
    ny = 1
    while (2 * ny) ** 2 <= nb:
        ny *= 2
    nz = nb // ny

    def body(features, w_first, bn_gain, bn_shift, w_second, prototypes, partner):
        rows, d_in = features.shape
        units, emb = w_second.shape
        protos = prototypes.shape[0]
        chunks = 8
        width = protos // chunks
        half = width // 2
        lanes = 128
        block = rows // npr
        slab, piece = d_in // ny, d_in // nb
        vmem = pltpu.VMEM
        scratch = dict(
            f=vmem((rows, d_in), bf16),
            w1=vmem((d_in, units), bf16),
            gain=vmem((1, units), f32),
            shift=vmem((1, units), f32),
            partner=vmem((1, rows), jnp.int32),
            w2=vmem((units, emb), bf16),
            pr=vmem((chunks, width, emb), bf16),
            u=vmem((chunks, width, emb), bf16),
            ft=vmem((ny, slab, 2 * rows), bf16),
            pair=vmem((2, 2 * rows, units), bf16),
            pre=vmem((rows, units), f32),
            mom=vmem((2, units), f32),
            mom_y=vmem((ny, 2, units), f32),
            mom2=vmem((2, units), f32),
            mom_z=vmem((nz, 2, units), f32),
            fsum=vmem((1, d_in), f32),
            fsum_y=vmem((ny, 1, d_in), f32),
            fsum2=vmem((1, d_in), f32),
            fsum_z=vmem((nz, 1, d_in), f32),
            fsum_own=vmem((piece, lanes), f32),
            fna=vmem((ny, nz, piece, lanes), f32),
            fnb=vmem((nz, ny, piece, lanes), f32),
            fna_y=vmem((ny - 2, nz, piece, lanes), f32),
            fnb_z=vmem((nz - 2, ny, piece, lanes), f32),
            fnas=vmem((nz, piece, lanes), f32),
            fnbs=vmem((ny, piece, lanes), f32),
            fna_z=vmem((nz, piece, lanes), f32),
            fnb_y=vmem((ny, piece, lanes), f32),
            fn_own=vmem((piece, units), f32),
            normed=vmem((rows, units), f32),
            shifted=vmem((rows, units), f32),
            hidden=vmem((rows, units), bf16),
            emb_part=vmem((npr, block, emb), f32),
            emb_rs=vmem((npr, block, emb), f32),
            emb_own=vmem((block, emb), f32),
            emb_ag=vmem((npr, block, emb), f32),
            embedded=vmem((rows, emb), f32),
            emb_low=vmem((rows, emb), bf16),
            inv_norm=vmem((rows, lanes), f32),
            codes=vmem((chunks, rows, width), f32),
            raised=vmem((chunks, rows, width), bf16),
            col_a=vmem((ITERS, chunks, half), f32),
            col_b=vmem((ITERS, chunks, half), f32),
            col_a1=vmem((ITERS, ny, chunks, half), f32),
            col_b1=vmem((ITERS, nz, chunks, half), f32),
            col_as=vmem((ITERS, chunks, half), f32),
            col_bs=vmem((ITERS, chunks, half), f32),
            col_a2=vmem((ITERS, nz, chunks, half), f32),
            col_b2=vmem((ITERS, ny, chunks, half), f32),
            scale_a=vmem((chunks, half), f32),
            scale_b=vmem((chunks, half), f32),
            soft_part=vmem((npr, block, emb), f32),
            soft_rs=vmem((npr, block, emb), f32),
            soft_own=vmem((block, emb), f32),
            soft_ag=vmem((npr, block, emb), f32),
            row_src=vmem((ITERS - 1, 2, rows), f32),
            row_ag=vmem((ITERS - 1, npr, 2, rows), f32),
            denom=vmem((1, rows), f32),
            scale_rows=vmem((rows, lanes), f32),
            tgt_part=vmem((npr, block, emb), f32),
            tgt_rs=vmem((npr, block, emb), f32),
            tgt_own=vmem((block, emb), f32),
            tgt_ag=vmem((npr, block, emb), f32),
            row_last=vmem((1, rows), f32),
            row_last_ag=vmem((npr, 1, rows), f32),
            gsum=vmem((2, units), f32),
            gsum_y=vmem((ny, 2, units), f32),
            gsum2=vmem((2, units), f32),
            gsum_z=vmem((nz, 2, units), f32),
            g2a=vmem((ny, nz // 2, 8, lanes), f32),
            g2b=vmem((nz // 2, 2, ny // 2, 8, lanes), f32),
            g2a_y=vmem((ny, nz // 2, 8, lanes), f32),
            g2b_z=vmem((nz, ny // 2, 8, lanes), f32),
            g2as=vmem((nz // 2, 8, lanes), f32),
            g2bs=vmem((ny // 2, 8, lanes), f32),
            g2a_z=vmem((nz, 8, lanes), f32),
            g2b_y=vmem((ny, 8, lanes), f32),
            g1a_r=vmem((nz, piece, lanes), f32),
            g1b_r=vmem((ny, piece, lanes), f32),
            fna_r=vmem((nz, piece, lanes), f32),
            fnb_r=vmem((ny, piece, lanes), f32),
            g1a=vmem((ny, nz, piece, lanes), f32),
            g1b=vmem((nz, ny, piece, lanes), f32),
            g1a_y=vmem((ny - 2, nz, piece, lanes), f32),
            g1b_z=vmem((nz - 2, ny, piece, lanes), f32),
            g1as=vmem((nz, piece, lanes), f32),
            g1bs=vmem((ny, piece, lanes), f32),
            g1a_z=vmem((nz, piece, lanes), f32),
            g1b_y=vmem((ny, piece, lanes), f32),
            send_sem=pltpu.SemaphoreType.DMA((64,)),
            recv_sem=pltpu.SemaphoreType.DMA((64,)),
            in_sem=pltpu.SemaphoreType.DMA((7,)),
        )
        whole = pl.BlockSpec(memory_space=pl.ANY)
        here = pl.BlockSpec(memory_space=pltpu.VMEM)
        inputs = dict(
            f_in=features,
            w1_in=w_first,
            gain_in=bn_gain.reshape(1, units),
            shift_in=bn_shift.reshape(1, units),
            w2_in=w_second,
            pr_in=prototypes.reshape(chunks, width, emb),
            partner_in=partner.reshape(1, rows),
        )
        outputs = dict(
            penalty=jax.ShapeDtypeStruct((1, rows), f32),
            grad_w1=jax.ShapeDtypeStruct((piece, units), f32),
            grad_gain=jax.ShapeDtypeStruct((1, units), f32),
            grad_shift=jax.ShapeDtypeStruct((1, units), f32),
            grad_w2=jax.ShapeDtypeStruct((emb // nb, units), f32),
        )
        names = tuple(inputs) + tuple(outputs) + tuple(scratch)
        results = pl.pallas_call(
            make_kernel(ny, nz, npr, names, float(rows * nb)),
            out_shape=tuple(outputs.values()),
            in_specs=[whole] * len(inputs),
            out_specs=[here] * len(outputs),
            scratch_shapes=list(scratch.values()),
            compiler_params=pltpu.CompilerParams(
                collective_id=0, has_side_effects=True, vmem_limit_bytes=60 << 20
            ),
            name="head_step",
        )(*inputs.values())
        penalty, grad_w1, grad_gain, grad_shift, grad_w2 = pl.pallas_call(
            hand_over,
            out_shape=tuple(outputs.values()),
            in_specs=[whole] * len(outputs),
            out_specs=[whole] * len(outputs),
            scratch_shapes=[pltpu.SemaphoreType.DMA((len(outputs),))],
            name="hand_over",
        )(*results)
        return (
            penalty.reshape(rows),
            grad_w1,
            grad_gain.reshape(units),
            grad_shift.reshape(units),
            grad_w2.T,
        )

    return jax.shard_map(
        body,
        mesh=mesh,
        in_specs=(
            P("batch", None),
            P(None, "proto"),
            P("proto"),
            P("proto"),
            P("proto", None),
            P("proto", None),
            P("batch"),
        ),
        out_specs=(P("batch"), P("batch", "proto"), P("proto"), P("proto"), P("proto", "batch")),
        check_vma=False,
    )
```

time: 1660 us -> 138 us (0.08)
  blocking collectives: 1150 us -> 0 us
  waiting for transfers between devices: 438 us -> 0 us
  Pallas kernels: 0 us -> 136 us
  matrix products: 31.9 us -> 0 us
    psum x8 -> x0, blocking collectives: 1150 us -> none  [the longest x5 912 us: batch_sums(): return lax.psum(values, 'batch')]
    psum x2 -> x0, waiting for transfers between devices: 247 us -> none  [proto_sums(): return lax.psum(values, 'proto')]
    unnamed x4 -> x0, waiting for transfers between devices: 191 us -> none
    pallas_call x0 -> x2, Pallas kernels: none -> 136 us  [the longest x1 134 us: body(): pl.pallas_call(make_kernel(ny, nz, npr, names, float(rows * nb)), out_sha...]
    dot_general x13 -> x0, matrix products: 31.9 us -> none  [the longest x3 10.2 us: body(): jnp.dot(exponent_codes, scale_cols, precision=highest)]
  transfers between devices with their start and end apart: 3 -> 0, of which waited for: 3 -> 0; matrix products, arithmetic and copies ran while one was open for 0% -> 0% of each run, Pallas kernels for 0% -> 0%
where the time goes in v1:
time: 138 us; the launch traced here: 136 us
  Pallas kernels  136 us (99%)
    pallas_call x1, Pallas kernels, body(): pl.pallas_call(make_kernel(ny, nz, npr, names, float(rows * nb)), out_sha...  134 us

profile of v1, /device:TPU:1, one launch (start us, length us, event | category | flops | bytes accessed | tf_op | source)
XLA Modules:
  0.0 136.4 jit_solution(284482649207436252)
XLA Ops:
  0.6 133.7 %head_step.1 = (f32[1,128]{1,0:T(1,128)}, f32[24,256]{1,0:T(8,128)}, f32[1,256]{1,0:T(1,128)}, f32[1,256]{1,0:T(1,128)}, f32[4,256]{1,0:T(4,128)}) custom-call(bf16[128,1536]{1,0:T(8,128)(2,1)} %refs_0_.1, bf16[1536,256]{1,0:T(8,128)(2,1)} %refs_1_.1, f32[1,256]{1,0:T(1,128)} %bitcast.9, f32[1,256]{1,0:T(1,128)} %bitcast.10, bf16[256,256]{1,0:T(8,128)(2,1)} %refs_4_.1, ...), custom_call_target="tpu_custom_call" | custom-call | tf_op jit(solution)/shard_map/head_step/pallas_call | solution.py:573
  134.3 2.1 %hand_over.1 = (f32[1,128]{1,0:T(1,128)}, f32[24,256]{1,0:T(8,128)}, f32[1,256]{1,0:T(1,128)}, f32[1,256]{1,0:T(1,128)}, f32[4,256]{1,0:T(4,128)}) custom-call(f32[1,128]{1,0:T(1,128)} %get-tuple-element.15.refs_0_, f32[24,256]{1,0:T(8,128)} %get-tuple-element.16.refs_1_, f32[1,256]{1,0:T(1,128)} %get-tuple-element.17.refs_2_, ...), custom_call_target="tpu_custom_call" | custom-call | tf_op jit(solution)/shard_map/hand_over/pallas_call | solution.py:584

commit v2 on v1

--- a/solution.py
+++ b/solution.py
@@ -83,16 +83,20 @@
             count, me, device = rings[axis]
             far = count // 2
             stage_r, stage = new_stage(relay), new_stage(landing)
-            back = (me + count - 1) % count
-            send(source.at[(me + far) % count], relay, stage_r, device(back))
-            near = [o for d in range(far - 1, 0, -1) for o in (d, count - d) if o != far + 1]
+            turn = 1 - 2 * (proto % 2)
+
+            def member(offset):
+                return (me + turn * offset + count) % count
+
+            send(source.at[member(far)], relay, stage_r, device(member(-1)))
+            near = [o for d in range(far - 1, 0, -1) for o in (d, -d) if o != 1 - far]
             for slot, offset in enumerate(near):
-                peer = (me + offset) % count
+                peer = member(offset)
                 send(source.at[peer], landing.at[slot], stage, device(peer))
 
             def pass_on():
                 arrived(stage_r)
-                peer = (me + far + 1) % count
+                peer = member(1 - far)
                 source[peer] = source[peer] + relay[...]
                 send(source.at[peer], landing.at[len(near)], stage, device(peer))
 
@@ -101,6 +105,29 @@
                 return total(landing) + source[me]
 
             return pass_on, result
+
+        def sum_start(value, parts, landing):
+            begun = []
+            for h in range(2):
+                parts[h] = value[:, h * 128 : (h + 1) * 128].reshape(parts.shape[1:])
+                begun.append(exchange("p", lambda q: parts.at[h, q], landing.at[h]))
+            return begun
+
+        def sum_spread(begun, landing, own, everywhere):
+            spread = []
+            for h in range(2):
+                arrived(begun[h])
+                own[h] = total(landing.at[h])
+                spread.append(exchange("p", lambda q: own.at[h], everywhere.at[h]))
+            return spread
+
+        def sum_end(spread, everywhere):
+            sides = []
+            for h in range(2):
+                arrived(spread[h])
+                side = everywhere[h]
+                sides.append(side.reshape(side.shape[0] * side.shape[1], side.shape[2]))
+            return jnp.concatenate(sides, 1)
 
         loads = [
             pltpu.make_async_copy(src, dst, in_sem.at[i])
@@ -183,9 +210,7 @@
         r.hidden[...] = hidden
 
         part = jnp.dot(hidden, r.w2[...], preferred_element_type=f32)
-        r.emb_part[...] = part.reshape(r.emb_part.shape)
-        stage = exchange("p", lambda q: r.emb_part.at[q], r.emb_rs)
-
+        begun = sum_start(part, r.emb_part, r.emb_rs)
         chunks, width = r.u.shape[0], r.u.shape[1]
 
         def unit(j, carry):
@@ -197,15 +222,12 @@
         lax.fori_loop(0, chunks // 2, unit, 0)
         pass_a()
         pass_b()
-        arrived(stage)
-        r.emb_own[...] = total(r.emb_rs)
-        stage = exchange("p", lambda q: r.emb_own, r.emb_ag)
+        spread = sum_spread(begun, r.emb_rs, r.emb_own, r.emb_ag)
         lax.fori_loop(chunks // 2, chunks, unit, 0)
         arrived(stage_f)
         r.fsum2[...] = total(r.fsum_y)
         stage_f = exchange("z", lambda q: r.fsum2, r.fsum_z)
-        arrived(stage)
-        raw_emb = r.emb_ag[...].reshape(rows, emb)
+        raw_emb = sum_end(spread, r.emb_ag)
         inv_norm = lax.rsqrt(jnp.sum(raw_emb * raw_emb, 1, keepdims=True) + 1e-06)
         embedded = raw_emb * inv_norm
         emb_low = embedded.astype(bf16)
@@ -262,24 +284,12 @@
                     return acc + jnp.dot(r.raised[j], r.u[j], preferred_element_type=f32)
 
                 soft_part = lax.fori_loop(0, chunks, soft, jnp.zeros((rows, emb), f32))
-                r.soft_part[...] = soft_part.reshape(r.soft_part.shape)
-                soft_rs = exchange("p", lambda q: r.soft_part.at[q], r.soft_rs)
+                begun = sum_start(soft_part, r.soft_part, r.soft_rs)
                 r.row_src[0, 1:2, :] = to_row(denom_part)
             if it == 1:
-                arrived(soft_rs)
-                r.soft_own[...] = total(r.soft_rs)
-                soft_ag = exchange("p", lambda q: r.soft_own, r.soft_ag)
                 r.row_src[1, 1:2, :] = jnp.zeros((1, lanes), f32)
-                arrived(stage_f)
-                wanted = batch * piece + lax.broadcasted_iota(jnp.int32, (piece, ny * slab), 0)
-                here = lax.broadcasted_iota(jnp.int32, (piece, ny * slab), 1) == wanted
-                r.fsum_own[...] = jnp.broadcast_to(
-                    jnp.sum(jnp.where(here, total(r.fsum_z), 0.0), 1, keepdims=True), (piece, lanes)
-                )
                 r.fnas[...] = early_a()
                 stage_na = exchange("z", lambda q: r.fnas.at[q], r.fna_z)
-                r.fnbs[...] = early_b()
-                stage_nb = exchange("y", lambda q: r.fnbs.at[q], r.fnb_y)
             if it == 2:
                 arrived(stage_na)
                 r.fn_own[:, :lanes] = total(r.fna_z)
@@ -291,6 +301,9 @@
             arrived(stage_b)
             r.col_bs[it] = total(r.col_b1.at[it])
             stage_b = exchange("y", lambda q: r.col_bs.at[it], r.col_b2.at[it])
+            if it == 1:
+                r.fnbs[...] = early_b()
+                stage_nb = exchange("y", lambda q: r.fnbs.at[q], r.fnb_y)
             arrived(stage_a)
             r.scale_a[...] = 1.0 / total(r.col_a2.at[it])
             arrived(stage_b)
@@ -299,6 +312,15 @@
                 break
             r.row_src[it, 0:1, :] = row_sums(None)
             stage = exchange("p", lambda q: r.row_src.at[it], r.row_ag.at[it])
+            if it == 0:
+                soft_spread = sum_spread(begun, r.soft_rs, r.soft_own, r.soft_ag)
+            if it == 1:
+                arrived(stage_f)
+                wanted = batch * piece + lax.broadcasted_iota(jnp.int32, (piece, ny * slab), 0)
+                here = lax.broadcasted_iota(jnp.int32, (piece, ny * slab), 1) == wanted
+                r.fsum_own[...] = jnp.broadcast_to(
+                    jnp.sum(jnp.where(here, total(r.fsum_z), 0.0), 1, keepdims=True), (piece, lanes)
+                )
             arrived(stage)
             masses = total(r.row_ag.at[it])
             if it == 0:
@@ -336,14 +358,10 @@
         row_part, target_part = lax.fori_loop(
             0, chunks, target, (jnp.zeros((rows, lanes), f32), jnp.zeros((rows, emb), f32))
         )
-        r.tgt_part[...] = target_part.reshape(r.tgt_part.shape)
-        stage = exchange("p", lambda q: r.tgt_part.at[q], r.tgt_rs)
+        begun = sum_start(target_part, r.tgt_part, r.tgt_rs)
         r.row_last[...] = to_row(row_part)
         stage_r = exchange("p", lambda q: r.row_last, r.row_last_ag)
-        arrived(stage)
-        r.tgt_own[...] = total(r.tgt_rs)
-        stage = exchange("p", lambda q: r.tgt_own, r.tgt_ag)
-        arrived(soft_ag)
+        spread = sum_spread(begun, r.tgt_rs, r.tgt_own, r.tgt_ag)
         arrived(stage_r)
         scale_last = to_columns(1.0 / total(r.row_last_ag))
         denom = r.denom[...]
@@ -351,9 +369,8 @@
         rows_iota = lax.broadcasted_iota(jnp.int32, (rows, rows), 0)
         swap = jnp.where(r.partner[...] == rows_iota, 1.0, 0.0).astype(f32)
         wide = lambda x: jnp.concatenate([x, x], 1)
-        soft_grad = r.soft_ag[...].reshape(rows, emb) * wide(denom_columns)
-        arrived(stage)
-        own_target = r.tgt_ag[...].reshape(rows, emb) * wide(scale_last)
+        soft_grad = sum_end(soft_spread, r.soft_ag) * wide(denom_columns)
+        own_target = sum_end(spread, r.tgt_ag) * wide(scale_last)
         partner_target = jnp.dot(
             swap, own_target, precision=lax.Precision.HIGHEST, preferred_element_type=f32
         )
@@ -490,10 +507,10 @@
             normed=vmem((rows, units), f32),
             shifted=vmem((rows, units), f32),
             hidden=vmem((rows, units), bf16),
-            emb_part=vmem((npr, block, emb), f32),
-            emb_rs=vmem((npr, block, emb), f32),
-            emb_own=vmem((block, emb), f32),
-            emb_ag=vmem((npr, block, emb), f32),
+            emb_part=vmem((2, npr, block, emb // 2), f32),
+            emb_rs=vmem((2, npr, block, emb // 2), f32),
+            emb_own=vmem((2, block, emb // 2), f32),
+            emb_ag=vmem((2, npr, block, emb // 2), f32),
             embedded=vmem((rows, emb), f32),
             emb_low=vmem((rows, emb), bf16),
             inv_norm=vmem((rows, lanes), f32),
@@ -509,18 +526,18 @@
             col_b2=vmem((ITERS, ny, chunks, half), f32),
             scale_a=vmem((chunks, half), f32),
             scale_b=vmem((chunks, half), f32),
-            soft_part=vmem((npr, block, emb), f32),
-            soft_rs=vmem((npr, block, emb), f32),
-            soft_own=vmem((block, emb), f32),
-            soft_ag=vmem((npr, block, emb), f32),
+            soft_part=vmem((2, npr, block, emb // 2), f32),
+            soft_rs=vmem((2, npr, block, emb // 2), f32),
+            soft_own=vmem((2, block, emb // 2), f32),
+            soft_ag=vmem((2, npr, block, emb // 2), f32),
             row_src=vmem((ITERS - 1, 2, rows), f32),
             row_ag=vmem((ITERS - 1, npr, 2, rows), f32),
             denom=vmem((1, rows), f32),
             scale_rows=vmem((rows, lanes), f32),
-            tgt_part=vmem((npr, block, emb), f32),
-            tgt_rs=vmem((npr, block, emb), f32),
-            tgt_own=vmem((block, emb), f32),
-            tgt_ag=vmem((npr, block, emb), f32),
+            tgt_part=vmem((2, npr, block, emb // 2), f32),
+            tgt_rs=vmem((2, npr, block, emb // 2), f32),
+            tgt_own=vmem((2, block, emb // 2), f32),
+            tgt_ag=vmem((2, npr, block, emb // 2), f32),
             row_last=vmem((1, rows), f32),
             row_last_ag=vmem((npr, 1, rows), f32),
             gsum=vmem((2, units), f32),

time: 138 us -> 135 us (0.978); the launches traced: 136 us -> 135 us
  no operation moved by 1% of the time
where the time goes in v2:
time: 135 us
  Pallas kernels  135 us (100%)
    pallas_call x1, Pallas kernels, body(): pl.pallas_call(make_kernel(ny, nz, npr, names, float(rows * nb)), out_sha...  133 us

profile of v2, /device:TPU:1, one launch (start us, length us, event | category | flops | bytes accessed | tf_op | source)
XLA Modules:
  0.0 135.3 jit_solution(14242594269276538469)
XLA Ops:
  0.6 132.6 %head_step.1 = (f32[1,128]{1,0:T(1,128)}, f32[24,256]{1,0:T(8,128)}, f32[1,256]{1,0:T(1,128)}, f32[1,256]{1,0:T(1,128)}, f32[4,256]{1,0:T(4,128)}) custom-call(bf16[128,1536]{1,0:T(8,128)(2,1)} %refs_0_.1, bf16[1536,256]{1,0:T(8,128)(2,1)} %refs_1_.1, f32[1,256]{1,0:T(1,128)} %bitcast.9, f32[1,256]{1,0:T(1,128)} %bitcast.10, bf16[256,256]{1,0:T(8,128)(2,1)} %refs_4_.1, ...), custom_call_target="tpu_custom_call" | custom-call | tf_op jit(solution)/shard_map/head_step/pallas_call | solution.py:590
  133.2 2.1 %hand_over.1 = (f32[1,128]{1,0:T(1,128)}, f32[24,256]{1,0:T(8,128)}, f32[1,256]{1,0:T(1,128)}, f32[1,256]{1,0:T(1,128)}, f32[4,256]{1,0:T(4,128)}) custom-call(f32[1,128]{1,0:T(1,128)} %get-tuple-element.15.refs_0_, f32[24,256]{1,0:T(8,128)} %get-tuple-element.16.refs_1_, f32[1,256]{1,0:T(1,128)} %get-tuple-element.17.refs_2_, ...), custom_call_target="tpu_custom_call" | custom-call | tf_op jit(solution)/shard_map/hand_over/pallas_call | solution.py:601
